TPU v7x, 32 devices: a whole 2x2x4 slice. The times are simulated.
32 devices in a mesh: ctx: 2 (over y), section: 4 (over x, core), tp: 4 (over z).
Axes of the slice: x: 2, y: 2, z: 4, core: 2. Of those that a mesh axis runs over, the one named last changes fastest.
Arguments:
- queries: bfloat16 [256, 8192], P('ctx', ('section', 'tp')), may hold values from -140 to 140
- keys: bfloat16 [256, 1024], P('ctx', 'section'), may hold values from -6 to 6
- values: bfloat16 [256, 1024], P('ctx', 'section'), may hold values from -36 to 36
- out_grad: bfloat16 [256, 8192], P('ctx', ('section', 'tp')), may hold values from -6 to 6
- enc_weight: bfloat16 [8192, 65536], P(('section', 'tp'), 'ctx'), may hold values from -0.0625 to 0.0625
- enc_bias: float32 [65536], P(('ctx', 'section', 'tp')), may hold values from -3 to 3
- dec_weight: bfloat16 [65536, 8192], P('ctx', ('section', 'tp')), may hold values from -0.0625 to 0.0625
Outputs:
- query_grad: bfloat16 [256, 8192], P('ctx', ('section', 'tp'))
- gradient_keys: bfloat16 [256, 1024], P('ctx', 'section')
- gradient_values: bfloat16 [256, 1024], P('ctx', 'section')
- feature_scores: float32 [65536], P(('ctx', 'section', 'tp'))
All inputs are finite; a program needn't handle non-finite values.
Results may differ from a plain program's by a relative error of at most 0.015.
Values may be sent and summed in bfloat16 or wider, within the bound.
No kernel may reach another device: no remote copies, remote signals or barrier semaphores. Data moves between devices by JAX's collectives and lax.ppermute only.
A program may use at most 256 MiB of HBM per device.

v0:
```python
import math
import jax
import jax.numpy as jnp
from jax import lax
from jax.sharding import PartitionSpec as P

QUERY_HEADS = 64
KEY_VALUE_HEADS = 8
HEAD_SIZE = 128
D_Z = 8192
NEGATIVE = -1e30


def passed_along(value, axis, steps):
    count = lax.axis_size(axis)
    pairs = [(source, (source + steps) % count) for source in range(count)]
    return lax.ppermute(value, axis, pairs)


def spread(value, axis, root):
    mine = lax.axis_index(axis) == root
    return lax.psum(jnp.where(mine, value, jnp.zeros_like(value)), axis)


def token_positions(device, row_count, cycle_size):
    half = row_count // 2
    local = jnp.arange(row_count, dtype=jnp.int32)
    block = jnp.where(local >= half, 2 * cycle_size - 1 - device, device)
    return block * half + local % half


def causal_block(query_pos, anchor, row_count, cycle_size):
    key_pos = token_positions(anchor, row_count, cycle_size)
    return query_pos[:, None] >= key_pos[None, :]


def pass_gradients(key_acc, value_acc):
    return passed_along((key_acc, value_acc), "ctx", -1)


def body(queries, keys, values, out_grad, enc_weight, enc_bias, dec_weight):
    row_count = queries.shape[0]
    heads_here = queries.shape[1] // HEAD_SIZE
    kv_here = keys.shape[1] // HEAD_SIZE
    group_width = QUERY_HEADS // KEY_VALUE_HEADS
    score_scale = 1.0 / math.sqrt(HEAD_SIZE)
    cycle_size = lax.axis_size("ctx")
    cycle_index = lax.axis_index("ctx")
    local_kv = lax.axis_index("tp") * heads_here // group_width
    key_own = lax.dynamic_slice_in_dim(keys, local_kv * HEAD_SIZE, HEAD_SIZE, 1)
    value_own = lax.dynamic_slice_in_dim(values, local_kv * HEAD_SIZE, HEAD_SIZE, 1)
    query_heads = queries.reshape(row_count, heads_here, HEAD_SIZE)
    grad_heads = out_grad.reshape(row_count, heads_here, HEAD_SIZE)
    query_pos = token_positions(cycle_index, row_count, cycle_size)
    store_count = 1

    def block_logits(turn, key_blk):
        anchor = (cycle_index + turn) % cycle_size
        causal_mask = causal_block(query_pos, anchor, row_count, cycle_size)
        logits = (
            jnp.einsum("qhd,kd->hqk", query_heads, key_blk, preferred_element_type=jnp.float32)
            * score_scale
        )
        return (causal_mask, logits)

    def forward_turn(turn, loop_state):
        key_blk, value_blk, running_max, running_sum, running_out, key_store, value_store = (
            loop_state
        )
        causal_mask, logits = block_logits(turn, key_blk)
        logits = jnp.where(causal_mask[None], logits, NEGATIVE)
        new_max = jnp.maximum(running_max, jnp.max(logits, axis=2))
        weights = jnp.where(causal_mask[None], jnp.exp(logits - new_max[:, :, None]), 0.0)
        factor = jnp.exp(running_max - new_max)
        running_sum = running_sum * factor + jnp.sum(weights, axis=2)
        weights_high = weights.astype(jnp.bfloat16)
        weights_low = (weights - weights_high.astype(jnp.float32)).astype(jnp.bfloat16)
        block_out = jnp.einsum(
            "hqk,kd->hqd", weights_high, value_blk, preferred_element_type=jnp.float32
        )
        block_out = block_out + jnp.einsum(
            "hqk,kd->hqd", weights_low, value_blk, preferred_element_type=jnp.float32
        )
        running_out = running_out * factor[:, :, None] + block_out
        key_blk, value_blk = passed_along((key_blk, value_blk), "ctx", -1)
        return (key_blk, value_blk, new_max, running_sum, running_out, key_store, value_store)

    empty_store = jnp.zeros((store_count, row_count, HEAD_SIZE), jnp.bfloat16)
    start_state = (
        key_own,
        value_own,
        jnp.full((heads_here, row_count), NEGATIVE, jnp.float32),
        jnp.zeros((heads_here, row_count), jnp.float32),
        jnp.zeros((heads_here, row_count, HEAD_SIZE), jnp.float32),
        empty_store,
        empty_store,
    )
    final_state = lax.fori_loop(0, cycle_size, forward_turn, start_state)
    running_max, running_sum, running_out, key_store, value_store = final_state[2:]
    log_total = running_max + jnp.log(running_sum)
    head_out = jnp.transpose(
        (running_out / running_sum[:, :, None]).astype(jnp.bfloat16), (1, 0, 2)
    )
    attn_flat = head_out.reshape(row_count, heads_here * HEAD_SIZE)
    row_dots = jnp.sum(grad_heads.astype(jnp.float32) * head_out.astype(jnp.float32), axis=2).T

    def gradient_terms(turn, key_blk, value_blk):
        causal_mask, logits = block_logits(turn, key_blk)
        weights = jnp.where(causal_mask[None], jnp.exp(logits - log_total[:, :, None]), 0.0)
        value_term = jnp.einsum(
            "hqk,qhd->kd",
            weights.astype(jnp.bfloat16),
            grad_heads,
            preferred_element_type=jnp.float32,
        )
        weight_grad = jnp.einsum(
            "qhd,kd->hqk", grad_heads, value_blk, preferred_element_type=jnp.float32
        )
        logit_half = (weights * (weight_grad - row_dots[:, :, None])).astype(jnp.bfloat16)
        query_term = jnp.einsum(
            "hqk,kd->qhd", logit_half, key_blk, preferred_element_type=jnp.float32
        )
        key_term = jnp.einsum(
            "hqk,qhd->kd", logit_half, query_heads, preferred_element_type=jnp.float32
        )
        return (query_term, key_term, value_term)

    zero_block = jnp.zeros((row_count, HEAD_SIZE), jnp.float32)
    zero_query = jnp.zeros((row_count, heads_here, HEAD_SIZE), jnp.float32)

    def moving_turn(turn, loop_state):
        key_blk, value_blk, key_acc, value_acc, query_acc = loop_state
        query_term, key_term, value_term = gradient_terms(turn, key_blk, value_blk)
        key_blk, value_blk = passed_along((key_blk, value_blk), "ctx", -1)
        key_acc, value_acc = pass_gradients(key_acc + key_term, value_acc + value_term)
        return (key_blk, value_blk, key_acc, value_acc, query_acc + query_term)

    moved_state = lax.fori_loop(
        0, cycle_size, moving_turn, (key_own, value_own, zero_block, zero_block, zero_query)
    )
    key_acc, value_acc, query_acc = moved_state[2:]
    query_grad = (
        (query_acc * score_scale).reshape(row_count, heads_here * HEAD_SIZE).astype(jnp.bfloat16)
    )
    head_slot = (jnp.arange(kv_here, dtype=jnp.int32) == local_kv)[None, :, None]
    key_full = jnp.where(head_slot, (key_acc * score_scale)[:, None, :], 0.0).reshape(
        row_count, kv_here * HEAD_SIZE
    )
    value_full = jnp.where(head_slot, value_acc[:, None, :], 0.0).reshape(
        row_count, kv_here * HEAD_SIZE
    )
    key_sum, value_sum = lax.psum((key_full, value_full), "tp")
    last_index = cycle_size - 1
    scored_out, scored_grad = (
        spread(attn_flat, "ctx", last_index),
        spread(out_grad, "ctx", last_index),
    )
    wide_out = scored_out.astype(jnp.float32)
    squares = lax.psum(jnp.sum(wide_out * wide_out, axis=1), ("section", "tp"))
    row_norm = jnp.sqrt(squares / D_Z + 1e-06)
    encoded_part = jnp.dot(scored_out, enc_weight, preferred_element_type=jnp.float32)
    attrib_part = lax.dot_general(
        scored_grad, dec_weight, (((1,), (1,)), ((), ())), preferred_element_type=jnp.float32
    )
    encoded, attrib = (
        lax.psum_scatter(encoded_part, ("section", "tp"), scatter_dimension=1, tiled=True),
        lax.psum_scatter(attrib_part, ("section", "tp"), scatter_dimension=1, tiled=True),
    )
    active = jnp.maximum(encoded / row_norm[:, None] + enc_bias[None, :], 0.0)
    feature_scores = jnp.sum(active * attrib, axis=0)
    return (
        query_grad,
        key_sum.astype(jnp.bfloat16),
        value_sum.astype(jnp.bfloat16),
        feature_scores,
    )


def solution(mesh):
    placed = (
        P("ctx", ("section", "tp")),
        P("ctx", "section"),
        P("ctx", "section"),
        P("ctx", ("section", "tp")),
        P(("section", "tp"), "ctx"),
        P(("ctx", "section", "tp")),
        P("ctx", ("section", "tp")),
    )
    return jax.shard_map(
        body,
        mesh=mesh,
        in_specs=placed,
        out_specs=(
            P("ctx", ("section", "tp")),
            P("ctx", "section"),
            P("ctx", "section"),
            P(("ctx", "section", "tp")),
        ),
        check_vma=False,
    )
```

profile of v0, /device:TPU:0, one launch (start us, length us, event | category | flops | bytes accessed | tf_op | source)
XLA Modules:
  0.0 448.3 jit_solution(17951976722139428715)
XLA Ops:
  7.3 0.8 constant_dynamic-slice_fusion
  8.1 1.0 copy.18
  9.1 0.1 copy.22
  9.2 11.2 %while.54 = (s32[]{:T(128)}, bf16[128,128]{1,0:T(8,128)(2,1)S(1)}, bf16[128,128]{1,0:T(8,128)(2,1)S(1)}, f32[4,128]{1,0:T(4,128)S(1)}, f32[4,128]{1,0:T(4,128)S(...) while((s32[]{:T(128)}, bf16[128,128]{1,0:T(8,128)(2,1)S(1)}, ...), condition=%wide.region_3.4_spmd.clone.clone.clone, body=%wide.region_0.3_spmd.clone.clone.clone.sunk | while | flops 51598352 | bytes 2838894 | solution.py:98
  9.3 3.0 collective-permute-start
  12.3 0.1 collective-permute-start.1
  12.4 0.1 broadcast_compare_fusion.4
  12.5 0.2 fusion.96
  12.7 0.1 fusion.97
  12.8 0.2 fusion.99
  13.0 0.3 fusion.100
  13.3 0.9 collective-permute-done
  14.2 2.0 collective-permute-done.1
  16.2 0.3 collective-permute-start
  16.6 1.7 collective-permute-start.1
  18.3 0.1 broadcast_compare_fusion.4
  18.4 0.2 fusion.96
  18.6 0.1 fusion.97
  18.7 0.2 fusion.99
  18.9 0.3 fusion.100
  19.2 1.0 collective-permute-done
  20.1 0.4 collective-permute-done.1
  20.5 0.1 copy.21
  20.6 0.7 broadcast_select_fusion
  21.3 0.7 broadcast_select_fusion.1
  22.1 25.8 %all-reduce.5.cloned.1.call-done = (bf16[128,512]{1,0:T(8,128)(2,1)}, bf16[128,512]{0,1:T(8,128)(2,1)}) async-done(((bf16[128,512]{1,0:T(8,128)(2,1)}, bf16[128,512]{0,1:T(8,128)(2,1)}), (bf16[128,512]{1,0:T(8,128)(2,1)}, bf16[128,512]{0,1:T(8,128)(2,1)})) %all-reduce.5.cloned.1.call-update) | async-done | bytes 262160 | tf_op jit(solution)/shard_map/psum | solution.py:22
  47.8 21.1 %fusion.48 = f32[128,32768]{1,0:T(8,128)} fusion(bf16[128,512]{0,1:T(8,128)(2,1)} %get-tuple-element.839, bf16[512,32768]{1,0:T(8,128)(2,1)} %param.15), kind=kOutput, calls=%fused_computation.83 | convolution fusion | flops 4294967296 | bytes 50462720 | tf_op jit(solution)/shard_map/dot_general | solution.py:161
  69.1 24.8 %fusion.49 = f32[128,32768]{1,0:T(8,128)} fusion(bf16[128,512]{1,0:T(8,128)(2,1)S(1)} %copy-done.2, bf16[32768,512]{1,0:T(8,128)(2,1)} %param.17), kind=kOutput, calls=%fused_computation.84 | convolution fusion | flops 4294967296 | bytes 50462720 | tf_op jit(solution)/shard_map/dot_general | solution.py:162
  93.9 0.1 copy.20
  94.0 0.1 copy.23
  94.2 0.1 broadcast_bitcast_fusion
  94.3 16.7 %while.55 = (s32[]{:T(128)}, bf16[128,128]{1,0:T(8,128)(2,1)S(1)}, bf16[128,128]{1,0:T(8,128)(2,1)S(1)}, f32[128,128]{1,0:T(8,128)S(1)}, f32[128,128]{1,0:T(8,12...) while((s32[]{:T(128)}, bf16[128,128]{1,0:T(8,128)(2,1)S(1)}, ...), condition=%wide.region_6.7_spmd.clone.clone.clone, body=%wide.region_5.6_spmd.clone.clone.clone.sunk | while | flops 84527632 | bytes 3545556 | solution.py:138
  94.3 0.2 collective-permute-start.3
  94.6 1.9 collective-permute-start.2
  96.4 0.1 broadcast_compare_fusion.5
  96.5 0.2 fusion.113
  96.7 0.2 fusion.114
  96.9 0.2 fusion.115
  97.1 0.2 collective-permute-start.4
  97.4 0.2 fusion.116
  97.5 1.9 collective-permute-start.5
  99.5 0.2 fusion.117
  99.7 1.7 collective-permute-done.4
  101.5 0.7 collective-permute-done.5
  102.2 1.6 collective-permute-start.3
  103.7 0.5 collective-permute-start.2
  104.2 0.1 broadcast_compare_fusion.5
  104.3 0.2 fusion.113
  104.5 0.2 fusion.114
  104.7 0.2 fusion.115
  104.9 1.6 collective-permute-start.4
  106.5 0.2 fusion.116
  106.7 0.5 collective-permute-start.5
  107.2 0.2 fusion.117
  107.5 0.2 collective-permute-done.2
  107.7 1.6 collective-permute-done.4
  109.2 1.8 collective-permute-done.5
  111.2 33.0 %all-reduce.6 = (bf16[128,256]{1,0:T(8,128)(2,1)}, bf16[128,256]{1,0:T(8,128)(2,1)}) all-reduce(f32[128,256]{1,0:T(8,128)S(1)} %get-tuple-element.845, f32[128,256]{1,0:T(8,128)S(1)} %get-tuple-element.844), channel_id=1, replica_groups=mesh['ctx'=2,'section'=4,'tp'=4] {'tp'}, use_global_device_ids=true, to_apply=%region_7.8 | all-reduce | flops 65536 | bytes 393216 | tf_op jit(solution)/shard_map/psum | solution.py:152
  144.3 0.7 copy_bitcast_fusion
  144.9 0.1 multiply_reduce_fusion.1
  145.0 32.5 %psum.38 = f32[128]{0:T(128)S(1)} all-reduce(f32[128]{0:T(128)S(1)} %multiply_reduce_fusion.1), channel_id=1, replica_groups=mesh['ctx'=2,'section'=4,'tp'=4] {'section','tp'}, use_global_device_ids=true, to_apply=%region_12.13 | all-reduce | flops 128 | bytes 1024 | tf_op jit(solution)/shard_map/psum | solution.py:159
  177.5 79.6 %reduce-scatter.3.cloned.1.call-done = f32[128,2048]{1,0:T(8,128)} async-done(((f32[128,32768]{1,0:T(8,128)}), f32[128,2048]{1,0:T(8,128)}) %reduce-scatter.3.cloned.1.call-update) | async-done | bytes 1048592 | tf_op jit(solution)/shard_map/reduce_scatter | solution.py:166
  257.1 182.2 %reduce-scatter.5.cloned.1.call-done = f32[128,2048]{1,0:T(8,128)} async-done(((f32[128,32768]{1,0:T(8,128)}), f32[128,2048]{1,0:T(8,128)}) %reduce-scatter.5.cloned.1.call-update) | async-done | bytes 1048592 | tf_op jit(solution)/shard_map/reduce_scatter | solution.py:167
  439.4 2.4 multiply_reduce_fusion
  (55 shorter events, 0.6 us)
Async XLA Ops:
  7.2 40.6 %all-reduce.5.cloned.1.call-start = ((), (), s32[]{:S(2)}) async-start(), calls=%async_computation.4 | async-start | bytes 524288 | tf_op jit(solution)/shard_map/psum | solution.py:22
  9.3 4.9 %collective-permute-start = (bf16[128,128]{1,0:T(8,128)(2,1)S(1)}, bf16[128,128]{1,0:T(8,128)(2,1)S(1)}, u32[]{:S(2)}, u32[]{:S(2)}) collective-permute-start(bf16[128,128]{1,0:T(8,128)(2,1)S(1)} %copy.41), channel_id=1, source_target_pairs={{0,16},{16,0},{1,17},{17,1},{2,18},{18,2},{3,19},{19,3},{4,20},{20... | collective-permute-start | bytes 98312 | tf_op jit(solution)/shard_map/while/body/eval_jaxpr/ppermute | solution.py:17
  12.3 3.9 collective-permute-start.1
  16.2 3.9 collective-permute-start
  16.6 3.9 collective-permute-start.1
  22.0 235.1 %reduce-scatter.3.cloned.1.call-start = ((), (), s32[]{:S(2)}) async-start(), calls=%async_computation.2 | async-start | bytes 17825792 | tf_op jit(solution)/shard_map/reduce_scatter | solution.py:166
  47.8 21.2 %copy-start.2 = (bf16[128,512]{1,0:T(8,128)(2,1)S(1)}, bf16[128,512]{1,0:T(8,128)(2,1)}, u32[]{:S(2)}) copy-start(bf16[128,512]{1,0:T(8,128)(2,1)} %get-tuple-element.838) | copy-start | bytes 393220
  69.0 370.4 %reduce-scatter.5.cloned.1.call-start = ((), (), s32[]{:S(2)}) async-start(), calls=%async_computation.3 | async-start | bytes 17825792 | tf_op jit(solution)/shard_map/reduce_scatter | solution.py:167
  69.0 24.8 %copy-start.1 = (bf16[128,512]{1,0:T(8,128)(2,1)S(1)}, bf16[128,512]{1,0:T(8,128)(2,1)}, u32[]{:S(2)}) copy-start(bf16[128,512]{1,0:T(8,128)(2,1)} %param.14) | copy-start | bytes 393220
  69.0 75.9 %copy-start = (bf16[128,512]{0,1:T(8,128)(2,1)S(1)}, bf16[128,512]{0,1:T(8,128)(2,1)}, u32[]{:S(2)}) copy-start(bf16[128,512]{0,1:T(8,128)(2,1)} %get-tuple-element.839) | copy-start | bytes 393220
  69.1 370.3 %copy-start.3 = (f32[2048]{0:T(1024)S(1)}, f32[2048]{0:T(1024)}, u32[]{:S(2)}) copy-start(f32[2048]{0:T(1024)} %param.16) | copy-start | bytes 24580
  94.3 5.4 %collective-permute-start.3 = (bf16[128,128]{1,0:T(8,128)(2,1)S(1)}, bf16[128,128]{1,0:T(8,128)(2,1)S(1)}, u32[]{:S(2)}, u32[]{:S(2)}) collective-permute-start(bf16[128,128]{1,0:T(8,128)(2,1)S(1)} %copy.60), channel_id=1, source_target_pairs={{0,16},{16,0},{1,17},{17,1},{2,18},{18,2},{3,19},{19,3},{4,20},{20... | collective-permute-start | bytes 98312 | tf_op jit(solution)/shard_map/while/body/eval_jaxpr/ppermute | solution.py:17
  94.6 5.2 %collective-permute-start.2 = (bf16[128,128]{1,0:T(8,128)(2,1)S(1)}, bf16[128,128]{1,0:T(8,128)(2,1)S(1)}, u32[]{:S(2)}, u32[]{:S(2)}) collective-permute-start(bf16[128,128]{1,0:T(8,128)(2,1)S(1)} %copy.59), channel_id=1, source_target_pairs={{0,16},{16,0},{1,17},{17,1},{2,18},{18,2},{3,19},{19,3},{4,20},{20... | collective-permute-start | bytes 98312 | tf_op jit(solution)/shard_map/while/body/eval_jaxpr/ppermute | solution.py:17
  97.1 4.3 collective-permute-start.4
  97.5 4.6 %collective-permute-start.5 = (f32[128,128]{1,0:T(8,128)S(1)}, f32[128,128]{1,0:T(8,128)S(1)}, u32[]{:S(2)}, u32[]{:S(2)}) collective-permute-start(f32[128,128]{1,0:T(8,128)S(1)} %fusion.116), channel_id=1, source_target_pairs={{0,16},{16,0},{1,17},{17,1},{2,18},{18,2},{3,19},{19,3},{4,20},{20... | collective-permute-start | bytes 196616 | tf_op jit(solution)/shard_map/while/body/eval_jaxpr/ppermute | solution.py:17
  102.2 5.3 %collective-permute-start.3 = (bf16[128,128]{1,0:T(8,128)(2,1)S(1)}, bf16[128,128]{1,0:T(8,128)(2,1)S(1)}, u32[]{:S(2)}, u32[]{:S(2)}) collective-permute-start(bf16[128,128]{1,0:T(8,128)(2,1)S(1)} %copy.60), channel_id=1, source_target_pairs={{0,16},{16,0},{1,17},{17,1},{2,18},{18,2},{3,19},{19,3},{4,20},{20... | collective-permute-start | bytes 98312 | tf_op jit(solution)/shard_map/while/body/eval_jaxpr/ppermute | solution.py:17
  103.7 3.9 collective-permute-start.2
  104.9 4.3 collective-permute-start.4
  106.7 4.3 collective-permute-start.5
Sparse Core Ops, SparseCore 0:
  22.1 25.6 all-reduce.4
  69.1 187.9 reduce-scatter.2
  261.8 177.5 reduce-scatter.4
where the time goes:
time: 449 us; the launch traced here: 448 us
  waiting for transfers between devices  298 us (66%)
  blocking collectives  65.5 us (15%)
  matrix products  49.3 us (11%)
  between operations  13.9 us (3%)
  starting transfers between devices  13.7 us (3%)
  other arithmetic  5.2 us (1%)
    reduce_scatter x1, waiting for transfers between devices, body(): lax.psum_scatter(attrib_part, ('section', 'tp'), scatter_dimension=1, til...  182 us
    reduce_scatter x1, waiting for transfers between devices, body(): lax.psum_scatter(encoded_part, ('section', 'tp'), scatter_dimension=1, ti...  79.6 us
    psum x1, blocking collectives, body(): key_sum, value_sum = lax.psum((key_full, value_full), 'tp')  33 us
    psum x1, blocking collectives, body(): squares = lax.psum(jnp.sum(wide_out * wide_out, axis=1), ('section', 'tp'))  32.5 us
    psum x1, waiting for transfers between devices, spread(): return lax.psum(jnp.where(mine, value, jnp.zeros_like(value)), axis)  25.8 us
    dot_general x1, matrix products, body(): lax.dot_general(scored_grad, dec_weight, (((1,), (1,)), ((), ())), prefer...  24.8 us
    dot_general x1, matrix products, body(): jnp.dot(scored_out, enc_weight, preferred_element_type=jnp.float32)  21.1 us
    ppermute x12, starting transfers between devices, passed_along(): return lax.ppermute(value, axis, pairs)  13.6 us
  transfers between devices with their start and end apart: 15, of which 12 were waited for; matrix products, arithmetic and copies ran while one was open for 7% of the time, Pallas kernels for 0%

commit v1 on v0

--- a/solution.py
+++ b/solution.py
@@ -19,7 +19,7 @@
 
 def spread(value, axis, root):
     mine = lax.axis_index(axis) == root
-    return lax.psum(jnp.where(mine, value, jnp.zeros_like(value)), axis)
+    return jnp.sum(lax.all_gather(jnp.where(mine, value, jnp.zeros_like(value)), axis), axis=0)
 
 
 def token_positions(device, row_count, cycle_size):

time: 449 us -> 428 us (0.953)
  waiting for transfers between devices: 298 us -> 265 us
  blocking collectives: 65.5 us -> 77.2 us
    psum x1 -> x0, waiting for transfers between devices: 25.8 us -> none  [spread(): return lax.psum(jnp.where(mine, value, jnp.zeros_like(value)), axis)]
    all_gather x0 -> x2, blocking collectives: none -> 11.3 us  [spread(): lax.all_gather(jnp.where(mine, value, jnp.zeros_like(value)), axis)]
    reduce_scatter x1, waiting for transfers between devices: 79.6 us -> 73.1 us  [body(): lax.psum_scatter(encoded_part, ('section', 'tp'), scatter_dimension=1, ti...]
  transfers between devices with their start and end apart: 15 -> 14, of which waited for: 12 -> 11; matrix products, arithmetic and copies ran while one was open for 7% -> 7% of each run, Pallas kernels for 0% -> 0%
where the time goes in v1:
time: 428 us
  waiting for transfers between devices  265 us (62%)
  blocking collectives  77.2 us (18%)
  matrix products  50.5 us (12%)
  between operations  14.3 us (3%)
  starting transfers between devices  13.7 us (3%)
    reduce_scatter x1, waiting for transfers between devices, body(): lax.psum_scatter(attrib_part, ('section', 'tp'), scatter_dimension=1, til...  182 us
    reduce_scatter x1, waiting for transfers between devices, body(): lax.psum_scatter(encoded_part, ('section', 'tp'), scatter_dimension=1, ti...  73.1 us
    psum x1, blocking collectives, body(): squares = lax.psum(jnp.sum(wide_out * wide_out, axis=1), ('section', 'tp'))  34.3 us
    psum x1, blocking collectives, body(): key_sum, value_sum = lax.psum((key_full, value_full), 'tp')  31.6 us
    dot_general x1, matrix products, body(): lax.dot_general(scored_grad, dec_weight, (((1,), (1,)), ((), ())), prefer...  26.3 us
    dot_general x1, matrix products, body(): jnp.dot(scored_out, enc_weight, preferred_element_type=jnp.float32)  20.8 us
    ppermute x12, starting transfers between devices, passed_along(): return lax.ppermute(value, axis, pairs)  13.6 us
    all_gather x2, blocking collectives, spread(): lax.all_gather(jnp.where(mine, value, jnp.zeros_like(value)), axis)  11.3 us
  transfers between devices with their start and end apart: 14, of which 11 were waited for; matrix products, arithmetic and copies ran while one was open for 7% of the time, Pallas kernels for 0%

profile of v1, /device:TPU:0, one launch (start us, length us, event | category | flops | bytes accessed | tf_op | source)
XLA Modules:
  0.0 427.7 jit_solution(4431521242133067180)
XLA Ops:
  7.3 0.8 constant_dynamic-slice_fusion
  8.1 1.0 copy.28
  9.1 0.1 copy.32
  9.2 11.2 %while.54 = (s32[]{:T(128)}, bf16[128,128]{1,0:T(8,128)(2,1)S(1)}, bf16[128,128]{1,0:T(8,128)(2,1)S(1)}, f32[4,128]{1,0:T(4,128)S(1)}, f32[4,128]{1,0:T(4,128)S(...) while((s32[]{:T(128)}, bf16[128,128]{1,0:T(8,128)(2,1)S(1)}, ...), condition=%wide.region_3.4_spmd.clone.clone.clone, body=%wide.region_0.3_spmd.clone.clone.clone.sunk | while | flops 51598352 | bytes 2838894 | solution.py:98
  9.3 3.0 collective-permute-start
  12.3 0.1 collective-permute-start.1
  12.4 0.1 broadcast_compare_fusion.4
  12.5 0.2 fusion.96
  12.7 0.1 fusion.97
  12.8 0.2 fusion.99
  13.0 0.3 fusion.100
  13.3 0.9 collective-permute-done
  14.2 2.0 collective-permute-done.1
  16.2 0.3 collective-permute-start
  16.6 1.7 collective-permute-start.1
  18.3 0.1 broadcast_compare_fusion.4
  18.4 0.2 fusion.96
  18.7 0.2 fusion.99
  18.9 0.3 fusion.100
  19.2 1.0 collective-permute-done
  20.1 0.4 collective-permute-done.1
  20.5 0.1 copy.31
  20.7 0.1 copy.35
  20.8 5.6 %all_gather.10 = bf16[2,128,512]{2,1,0:T(8,128)(2,1)S(1)} all-gather(bf16[1,128,512]{2,1,0:T(8,128)(2,1)S(1)} %copy.35), channel_id=1, replica_groups=mesh['ctx'=2,'section'=4,'tp'=4] {'ctx'}, dimensions={0}, use_global_device_ids=true | all-gather | bytes 393216 | tf_op jit(solution)/shard_map/all_gather | solution.py:22
  26.5 20.8 %fusion.48 = f32[128,32768]{1,0:T(8,128)} fusion(bf16[128,512]{1,0:T(8,128)(2,1)S(1)} %reduce_sum.69, bf16[512,32768]{1,0:T(8,128)(2,1)} %param.15), kind=kOutput, calls=%fused_computation.83 | convolution fusion | flops 4294967296 | bytes 50462720 | tf_op jit(solution)/shard_map/dot_general | solution.py:161
  47.4 5.6 %all-gather = bf16[256,512]{1,0:T(8,128)(2,1)S(1)} all-gather(bf16[128,512]{1,0:T(8,128)(2,1)S(1)} %broadcast_select_fusion), channel_id=2, replica_groups=mesh['ctx'=2,'section'=4,'tp'=4] {'ctx'}, dimensions={0}, use_global_device_ids=true | all-gather | bytes 393216 | tf_op jit(solution)/shard_map/all_gather | solution.py:22
  53.1 26.3 %fusion.49 = f32[128,32768]{1,0:T(8,128)} fusion(bf16[128,512]{1,0:T(8,128)(2,1)S(1)} %reduce_sum.71, bf16[32768,512]{1,0:T(8,128)(2,1)} %param.17), kind=kOutput, calls=%fused_computation.84 | convolution fusion | flops 4294967296 | bytes 50462720 | tf_op jit(solution)/shard_map/dot_general | solution.py:162
  79.5 0.1 copy.30
  79.6 0.1 copy.40
  79.8 0.1 copy.33
  80.0 0.1 broadcast_bitcast_fusion
  80.1 16.8 %while.55 = (s32[]{:T(128)}, bf16[128,128]{1,0:T(8,128)(2,1)S(1)}, bf16[128,128]{1,0:T(8,128)(2,1)S(1)}, f32[128,128]{1,0:T(8,128)S(1)}, f32[128,128]{1,0:T(8,12...) while((s32[]{:T(128)}, bf16[128,128]{1,0:T(8,128)(2,1)S(1)}, ...), condition=%wide.region_6.7_spmd.clone.clone.clone, body=%wide.region_5.6_spmd.clone.clone.clone.sunk | while | flops 84527632 | bytes 3545556 | solution.py:138
  80.1 1.7 collective-permute-start.3
  81.8 0.4 collective-permute-start.2
  82.2 0.1 broadcast_compare_fusion.5
  82.3 0.2 fusion.113
  82.5 0.2 fusion.114
  82.7 0.2 fusion.115
  82.9 1.7 collective-permute-start.4
  84.6 0.2 fusion.116
  84.8 0.5 collective-permute-start.5
  85.3 0.2 fusion.117
  85.5 0.5 collective-permute-done.2
  86.0 1.4 collective-permute-done.4
  87.4 1.7 collective-permute-done.5
  89.1 0.5 collective-permute-start.3
  89.6 1.6 collective-permute-start.2
  91.2 0.1 broadcast_compare_fusion.5
  91.3 0.2 fusion.113
  91.5 0.2 fusion.114
  91.7 0.2 fusion.115
  91.9 0.5 collective-permute-start.4
  92.4 0.2 fusion.116
  92.6 1.6 collective-permute-start.5
  94.2 0.2 fusion.117
  94.5 1.7 collective-permute-done.4
  96.2 0.7 collective-permute-done.5
  97.1 0.1 multiply_reduce_fusion.1
  97.1 34.3 %psum.23 = f32[128]{0:T(128)S(1)} all-reduce(f32[128]{0:T(128)S(1)} %multiply_reduce_fusion.1), channel_id=1, replica_groups=mesh['ctx'=2,'section'=4,'tp'=4] {'section','tp'}, use_global_device_ids=true, to_apply=%region_12.13 | all-reduce | flops 128 | bytes 1024 | tf_op jit(solution)/shard_map/psum | solution.py:159
  131.4 31.6 %all-reduce.2 = (bf16[128,256]{1,0:T(8,128)(2,1)}, bf16[128,256]{1,0:T(8,128)(2,1)}) all-reduce(f32[128,256]{1,0:T(8,128)S(1)} %get-tuple-element.864, f32[128,256]{1,0:T(8,128)S(1)} %get-tuple-element.863), channel_id=1, replica_groups=mesh['ctx'=2,'section'=4,'tp'=4] {'tp'}, use_global_device_ids=true, to_apply=%region_7.8 | all-reduce | flops 65536 | bytes 393216 | tf_op jit(solution)/shard_map/psum | solution.py:152
  163.0 0.7 copy_bitcast_fusion
  163.7 73.1 %reduce-scatter.3.cloned.1.call-done = f32[128,2048]{1,0:T(8,128)} async-done(((f32[128,32768]{1,0:T(8,128)}), f32[128,2048]{1,0:T(8,128)}) %reduce-scatter.3.cloned.1.call-update) | async-done | bytes 1048592 | tf_op jit(solution)/shard_map/reduce_scatter | solution.py:166
  236.8 181.7 %reduce-scatter.5.cloned.1.call-done = f32[128,2048]{1,0:T(8,128)} async-done(((f32[128,32768]{1,0:T(8,128)}), f32[128,2048]{1,0:T(8,128)}) %reduce-scatter.5.cloned.1.call-update) | async-done | bytes 1048592 | tf_op jit(solution)/shard_map/reduce_scatter | solution.py:167
  418.5 2.4 multiply_reduce_fusion
  (54 shorter events, 0.7 us)
Async XLA Ops:
  7.2 229.6 %reduce-scatter.3.cloned.1.call-start = ((), (), s32[]{:S(2)}) async-start(), calls=%async_computation.2 | async-start | bytes 17825792 | tf_op jit(solution)/shard_map/reduce_scatter | solution.py:166
  9.3 4.9 %collective-permute-start = (bf16[128,128]{1,0:T(8,128)(2,1)S(1)}, bf16[128,128]{1,0:T(8,128)(2,1)S(1)}, u32[]{:S(2)}, u32[]{:S(2)}) collective-permute-start(bf16[128,128]{1,0:T(8,128)(2,1)S(1)} %copy.54), channel_id=1, source_target_pairs={{0,16},{16,0},{1,17},{17,1},{2,18},{18,2},{3,19},{19,3},{4,20},{20... | collective-permute-start | bytes 98312 | tf_op jit(solution)/shard_map/while/body/eval_jaxpr/ppermute | solution.py:17
  12.3 3.9 collective-permute-start.1
  16.2 3.9 collective-permute-start
  16.6 3.9 collective-permute-start.1
  26.5 20.9 %copy-start = (bf16[128,512]{1,0:T(8,128)(2,1)S(1)}, bf16[128,512]{1,0:T(8,128)(2,1)}, u32[]{:S(2)}) copy-start(bf16[128,512]{1,0:T(8,128)(2,1)} %param.14) | copy-start | bytes 393220
  47.4 371.1 %reduce-scatter.5.cloned.1.call-start = ((), (), s32[]{:S(2)}) async-start(), calls=%async_computation.3 | async-start | bytes 17825792 | tf_op jit(solution)/shard_map/reduce_scatter | solution.py:167
  53.1 365.3 %copy-start.1 = (f32[2048]{0:T(1024)S(1)}, f32[2048]{0:T(1024)}, u32[]{:S(2)}) copy-start(f32[2048]{0:T(1024)} %param.16) | copy-start | bytes 24580
  80.1 5.4 %collective-permute-start.3 = (bf16[128,128]{1,0:T(8,128)(2,1)S(1)}, bf16[128,128]{1,0:T(8,128)(2,1)S(1)}, u32[]{:S(2)}, u32[]{:S(2)}) collective-permute-start(bf16[128,128]{1,0:T(8,128)(2,1)S(1)} %copy.73), channel_id=1, source_target_pairs={{0,16},{16,0},{1,17},{17,1},{2,18},{18,2},{3,19},{19,3},{4,20},{20... | collective-permute-start | bytes 98312 | tf_op jit(solution)/shard_map/while/body/eval_jaxpr/ppermute | solution.py:17
  81.8 4.2 collective-permute-start.2
  82.9 4.5 %collective-permute-start.4 = (f32[128,128]{1,0:T(8,128)S(1)}, f32[128,128]{1,0:T(8,128)S(1)}, u32[]{:S(2)}, u32[]{:S(2)}) collective-permute-start(f32[128,128]{1,0:T(8,128)S(1)} %fusion.115), channel_id=1, source_target_pairs={{0,16},{16,0},{1,17},{17,1},{2,18},{18,2},{3,19},{19,3},{4,20},{20... | collective-permute-start | bytes 196616 | tf_op jit(solution)/shard_map/while/body/eval_jaxpr/ppermute | solution.py:17
  84.8 4.3 %collective-permute-start.5 = (f32[128,128]{1,0:T(8,128)S(1)}, f32[128,128]{1,0:T(8,128)S(1)}, u32[]{:S(2)}, u32[]{:S(2)}) collective-permute-start(f32[128,128]{1,0:T(8,128)S(1)} %fusion.116), channel_id=1, source_target_pairs={{0,16},{16,0},{1,17},{17,1},{2,18},{18,2},{3,19},{19,3},{4,20},{20... | collective-permute-start | bytes 196616 | tf_op jit(solution)/shard_map/while/body/eval_jaxpr/ppermute | solution.py:17
  89.1 5.3 %collective-permute-start.3 = (bf16[128,128]{1,0:T(8,128)(2,1)S(1)}, bf16[128,128]{1,0:T(8,128)(2,1)S(1)}, u32[]{:S(2)}, u32[]{:S(2)}) collective-permute-start(bf16[128,128]{1,0:T(8,128)(2,1)S(1)} %copy.73), channel_id=1, source_target_pairs={{0,16},{16,0},{1,17},{17,1},{2,18},{18,2},{3,19},{19,3},{4,20},{20... | collective-permute-start | bytes 98312 | tf_op jit(solution)/shard_map/while/body/eval_jaxpr/ppermute | solution.py:17
  89.6 4.9 %collective-permute-start.2 = (bf16[128,128]{1,0:T(8,128)(2,1)S(1)}, bf16[128,128]{1,0:T(8,128)(2,1)S(1)}, u32[]{:S(2)}, u32[]{:S(2)}) collective-permute-start(bf16[128,128]{1,0:T(8,128)(2,1)S(1)} %copy.72), channel_id=1, source_target_pairs={{0,16},{16,0},{1,17},{17,1},{2,18},{18,2},{3,19},{19,3},{4,20},{20... | collective-permute-start | bytes 98312 | tf_op jit(solution)/shard_map/while/body/eval_jaxpr/ppermute | solution.py:17
  91.9 4.3 %collective-permute-start.4 = (f32[128,128]{1,0:T(8,128)S(1)}, f32[128,128]{1,0:T(8,128)S(1)}, u32[]{:S(2)}, u32[]{:S(2)}) collective-permute-start(f32[128,128]{1,0:T(8,128)S(1)} %fusion.115), channel_id=1, source_target_pairs={{0,16},{16,0},{1,17},{17,1},{2,18},{18,2},{3,19},{19,3},{4,20},{20... | collective-permute-start | bytes 196616 | tf_op jit(solution)/shard_map/while/body/eval_jaxpr/ppermute | solution.py:17
  92.6 4.3 %collective-permute-start.5 = (f32[128,128]{1,0:T(8,128)S(1)}, f32[128,128]{1,0:T(8,128)S(1)}, u32[]{:S(2)}, u32[]{:S(2)}) collective-permute-start(f32[128,128]{1,0:T(8,128)S(1)} %fusion.116), channel_id=1, source_target_pairs={{0,16},{16,0},{1,17},{17,1},{2,18},{18,2},{3,19},{19,3},{4,20},{20... | collective-permute-start | bytes 196616 | tf_op jit(solution)/shard_map/while/body/eval_jaxpr/ppermute | solution.py:17
Sparse Core Ops, SparseCore 0:
  47.5 189.2 reduce-scatter.2
  240.9 177.5 reduce-scatter.4
